TPU v7x, 256 devices: a whole 4x4x8 slice. The times are simulated.
256 devices in a mesh: tile: 64 (over x, y, z_lo, core), lev: 4 (over z_hi).
Axes of the slice: x: 4, y: 4, z: 8 (z_hi: 4, z_lo: 2; z = z_hi * 2 + z_lo), core: 2. Of those that a mesh axis runs over, the one named last changes fastest.
Arguments:
- adjoint_state: float32 [3, 16, 64, 128, 128], P(None, 'lev', 'tile'), may hold values from -6 to 6
- diffusivity: float32 [16, 64, 128, 128], P('lev', 'tile'), may hold values from 0.02 to 0.2
- retention: float32 [16, 64, 128, 128], P('lev', 'tile'), may hold values from 0 to 1, as said below
- coriolis: float32 [64, 128, 128], P('tile'), may hold values from -0.5 to 0.5
- neighbours: int32 [64, 4], replicated, may hold values from 0 to 63, as said below
- edge_from: int32 [64, 4], replicated, may hold values from 0 to 3
- rotation: int32 [64, 4], replicated, may hold values from 0 to 3
- seam_length: int32 [64, 4], replicated, may hold values from 32 to 128
- wet_mask: int32 [64, 128, 128], P('tile'), may hold values 0 or 1
Outputs:
- final_state: float32 [3, 16, 64, 128, 128], P(None, 'lev', 'tile')
Inputs may be any that keep to these rules, and one draw needn't show every extreme that they name: The four neighbours of a tile are four different tiles, never the tile itself. `retention`: every entry lies strictly between 0 and 1.
All inputs are finite; a program needn't handle non-finite values. No bound on the sum of `wet_mask` on one device may be relied on, other than what follows from the above.
Results may differ from a plain program's by a relative error of at most 0.0003.
Values sent between devices are 32-bit elements; how exact they have to be, the bound alone decides.
A program may use at most 64 MiB of HBM per device.

v0:
```python
import jax
import jax.numpy as jnp
from jax import lax
from jax.sharding import PartitionSpec as P

STEPS = 4


coupling = 0.25


def carried_in(x, axis, combine, identity):
    size, here = (lax.axis_size(axis), lax.axis_index(axis))
    everything = jax.tree.map(lambda part: lax.all_gather(part, axis), x)
    start = jax.tree.map(
        lambda part, zero: jnp.broadcast_to(jnp.asarray(zero, part.dtype), part.shape), x, identity
    )

    def step(k, before):
        at = size - 1 - k
        reached = at > here
        new = combine(before, jax.tree.map(lambda part: part[at], everything))
        return jax.tree.map(lambda a, b: jnp.where(reached, a, b), new, before)

    return lax.fori_loop(0, size, step, start)


def orient(strips, turns, seam_cells):
    size = strips.shape[-1]
    flipped = (turns == 1) | (turns == 2)
    strips = jnp.where(flipped, strips[..., ::-1], strips)
    cosine = (turns == 0).astype(jnp.float32) - (turns == 2).astype(jnp.float32)
    sine = (turns == 1).astype(jnp.float32) - (turns == 3).astype(jnp.float32)
    tracer = strips[0]
    zonal = strips[1]
    meridional = strips[2]
    new_zonal = cosine * zonal + sine * meridional
    new_meridional = cosine * meridional - sine * zonal
    inside = (lax.broadcasted_iota(jnp.int32, (size,), 0) < seam_cells).astype(jnp.float32)
    return jnp.stack([tracer * inside, new_zonal * inside, new_meridional * inside])


def edge_rows(state):
    return jnp.stack(
        [state[..., :, 0], state[..., :, -1], state[..., 0, :], state[..., -1, :]], axis=-2
    )


def pad_with(state, halo_rows):
    widths = [(0, 0)] * (state.ndim - 2) + [(1, 1), (1, 1)]
    padded = jnp.pad(state, widths)
    padded = padded.at[..., 1:-1, 0].set(halo_rows[..., 0, :])
    padded = padded.at[..., 1:-1, -1].set(halo_rows[..., 1, :])
    padded = padded.at[..., 0, 1:-1].set(halo_rows[..., 2, :])
    padded = padded.at[..., -1, 1:-1].set(halo_rows[..., 3, :])
    return padded


def advance(padded, diffusivity, coriolis, wet_cells):
    centre = padded[..., 1:-1, 1:-1]
    east_side = padded[..., 1:-1, 2:]
    west_side = padded[..., 1:-1, :-2]
    north_side = padded[..., 2:, 1:-1]
    south_side = padded[..., :-2, 1:-1]
    laplacian = east_side + west_side + north_side + south_side - 4.0 * centre
    tracer = centre[0]
    zonal = centre[1]
    meridional = centre[2]
    new_tracer = (
        tracer
        + diffusivity * laplacian[0]
        - coupling * 0.5 * (east_side[1] - west_side[1] + (north_side[2] - south_side[2]))
    )
    new_zonal = (
        zonal
        + diffusivity * laplacian[1]
        - coupling * 0.5 * (east_side[0] - west_side[0])
        + coriolis * meridional
    )
    new_meridional = (
        meridional
        + diffusivity * laplacian[2]
        - coupling * 0.5 * (north_side[0] - south_side[0])
        - coriolis * zonal
    )
    return jnp.stack([new_tracer * wet_cells, new_zonal * wet_cells, new_meridional * wet_cells])


def compose(deeper, upper):
    return (upper[0] * deeper[0], upper[1] + upper[0][None] * deeper[1])


def per_device(
    adjoint_state,
    diffusivity,
    retention,
    coriolis,
    neighbours,
    edge_from,
    rotation,
    seam_length,
    wet_mask,
):
    state = adjoint_state[:, :, 0]
    mixing = diffusivity[:, 0]
    weights = retention[:, 0]
    spin = coriolis[0]
    wet_cells = wet_mask[0].astype(jnp.float32)
    level_count = state.shape[1]
    own_tile = lax.axis_index("tile")
    neighbour_row = lax.dynamic_index_in_dim(neighbours, own_tile, 0, keepdims=False)
    source_row = lax.dynamic_index_in_dim(edge_from, own_tile, 0, keepdims=False)
    turn_row = lax.dynamic_index_in_dim(rotation, own_tile, 0, keepdims=False)
    seam_row = lax.dynamic_index_in_dim(seam_length, own_tile, 0, keepdims=False)
    for step in range(STEPS):
        outer_rows = edge_rows(state)
        everyone = lax.all_gather(outer_rows[None], "tile", axis=0, tiled=True)
        picked = jnp.moveaxis(everyone[neighbour_row, :, :, source_row, :], 0, 2)
        halo_rows = orient(picked, turn_row[:, None], seam_row[:, None])
        fresh = advance(pad_with(state, halo_rows), mixing, spin, wet_cells)
        carry = jnp.zeros_like(fresh[:, 0])
        product = jnp.ones_like(weights[0])
        partial_rows = [None] * level_count
        products = [None] * level_count
        for level in range(level_count - 1, -1, -1):
            carry = (1.0 - weights[level]) * fresh[:, level] + weights[level] * carry
            product = weights[level] * product
            partial_rows[level] = carry
            products[level] = product
        below = carried_in(
            (products[0], partial_rows[0]),
            "lev",
            compose,
            (jnp.ones_like(products[0]), jnp.zeros_like(partial_rows[0])),
        )
        incoming_level = below[1]
        state = jnp.stack(
            [
                partial_rows[level] + products[level][None] * incoming_level
                for level in range(level_count)
            ],
            axis=1,
        )
    return state[:, :, None]


def solution(mesh):
    in_specs = (
        P(None, "lev", "tile", None, None),
        P("lev", "tile", None, None),
        P("lev", "tile", None, None),
        P("tile", None, None),
        P(),
        P(),
        P(),
        P(),
        P("tile", None, None),
    )
    out_specs = P(None, "lev", "tile", None, None)
    return jax.shard_map(
        per_device, mesh=mesh, in_specs=in_specs, out_specs=out_specs, check_vma=False
    )
```

profile of v0, /device:TPU:1, one launch (start us, length us, event | category | flops | bytes accessed | tf_op | source)
XLA Modules:
  0.0 749.1 jit_solution(17224327549200517451)
XLA Ops:
  11.8 16.3 %all-gather.1 = f32[4,1,128,128]{3,2,1,0:T(8,128)S(1)} all-gather(f32[1,1,128,128]{3,2,1,0:T(8,128)S(1)} %get-tuple-element.1236), channel_id=3, replica_groups=mesh['tile'=64,'lev'=4] {'lev'}, dimensions={0}, use_global_device_ids=true | all-gather | bytes 327680 | tf_op jit(solution)/shard_map/all_gather | solution.py:14
  29.6 89.9 %all-gather.10.cloned.1.call-done = f32[192,4,4,128]{3,1,0,2:T(4,128)} async-done(((f32[3,4,4,128]{3,1,0,2:T(4,128)}), f32[192,4,4,128]{3,1,0,2:T(4,128)}) %all-gather.10.cloned.1.call-update) | async-done | bytes 1572880 | tf_op jit(solution)/shard_map/all_gather | solution.py:117
  119.4 2.8 copy.3430
  122.2 2.0 gather_fusion
  126.1 7.4 scatter.54
  133.5 33.5 %scatter.55 = f32[3,4,130,130]{3,1,0,2:T(4,128)S(1)} dynamic-update-slice(f32[3,4,130,130]{3,1,0,2:T(4,128)S(1)} %scatter.54, f32[3,4,128,1]{3,1,0,2:T(4,128)} %copy.3432, s32[]{:T(128)} %constant.573.clone.1, s32[]{:T(128)} %constant.573.clone.1, s32[]{:T(128)} %constant.575.clone.1, s32[]{:T(128)} %constant.579.clone.1) | dynamic-update-slice | bytes 12292 | tf_op jit(solution)/shard_map/scatter | solution.py:53
  173.3 18.9 %all_gather.19 = f32[4,3,128,128]{3,2,1,0:T(8,128)S(1)} all-gather(f32[1,3,128,128]{3,2,1,0:T(8,128)S(1)} %fusion.113), channel_id=1, replica_groups=mesh['tile'=64,'lev'=4] {'lev'}, dimensions={0}, use_global_device_ids=true | all-gather | bytes 983040 | tf_op jit(solution)/shard_map/all_gather | solution.py:14
  198.0 103.8 %all-gather.12.cloned.1.call-done = f32[192,4,4,128]{3,1,0,2:T(4,128)} async-done(((f32[3,4,4,128]{3,1,0,2:T(4,128)}), f32[192,4,4,128]{3,1,0,2:T(4,128)}) %all-gather.12.cloned.1.call-update) | async-done | bytes 1572880 | tf_op jit(solution)/shard_map/all_gather | solution.py:117
  301.9 2.8 copy.3448
  304.7 2.0 gather_fusion.1
  308.5 7.4 scatter.60
  316.0 33.5 %scatter.61 = f32[3,4,130,130]{3,1,0,2:T(4,128)S(1)} dynamic-update-slice(f32[3,4,130,130]{3,1,0,2:T(4,128)S(1)} %scatter.60, f32[3,4,128,1]{3,1,0,2:T(4,128)} %copy.3450, s32[]{:T(128)} %constant.573.clone.1, s32[]{:T(128)} %constant.573.clone.1, s32[]{:T(128)} %constant.575.clone.1, s32[]{:T(128)} %constant.579.clone.1) | dynamic-update-slice | bytes 12292 | tf_op jit(solution)/shard_map/scatter | solution.py:53
  355.8 18.9 %all_gather.42 = f32[4,3,128,128]{3,2,1,0:T(8,128)S(1)} all-gather(f32[1,3,128,128]{3,2,1,0:T(8,128)S(1)} %fusion.100), channel_id=1, replica_groups=mesh['tile'=64,'lev'=4] {'lev'}, dimensions={0}, use_global_device_ids=true | all-gather | bytes 983040 | tf_op jit(solution)/shard_map/all_gather | solution.py:14
  380.5 104.0 %all-gather.14.cloned.1.call-done = f32[192,4,4,128]{3,1,0,2:T(4,128)} async-done(((f32[3,4,4,128]{3,1,0,2:T(4,128)}), f32[192,4,4,128]{3,1,0,2:T(4,128)}) %all-gather.14.cloned.1.call-update) | async-done | bytes 1572880 | tf_op jit(solution)/shard_map/all_gather | solution.py:117
  484.5 2.8 copy.3465
  491.1 7.4 scatter.66
  498.5 33.5 %scatter.69 = f32[3,4,130,130]{3,1,0,2:T(4,128)S(1)} dynamic-update-slice(f32[3,4,130,130]{3,1,0,2:T(4,128)S(1)} %scatter.66, f32[3,4,128,1]{3,1,0,2:T(4,128)} %copy.3467, s32[]{:T(128)} %constant.573.clone.1, s32[]{:T(128)} %constant.573.clone.1, s32[]{:T(128)} %constant.575.clone.1, s32[]{:T(128)} %constant.579.clone.1) | dynamic-update-slice | bytes 12292 | tf_op jit(solution)/shard_map/scatter | solution.py:53
  538.3 18.9 %all_gather.44 = f32[4,3,128,128]{3,2,1,0:T(8,128)S(1)} all-gather(f32[1,3,128,128]{3,2,1,0:T(8,128)S(1)} %fusion.87), channel_id=1, replica_groups=mesh['tile'=64,'lev'=4] {'lev'}, dimensions={0}, use_global_device_ids=true | all-gather | bytes 983040 | tf_op jit(solution)/shard_map/all_gather | solution.py:14
  563.0 104.0 %all-gather.16.cloned.1.call-done = f32[192,4,4,128]{3,1,0,2:T(4,128)} async-done(((f32[3,4,4,128]{3,1,0,2:T(4,128)}), f32[192,4,4,128]{3,1,0,2:T(4,128)}) %all-gather.16.cloned.1.call-update) | async-done | bytes 1572880 | tf_op jit(solution)/shard_map/all_gather | solution.py:117
  667.1 2.8 copy.3482
  669.9 2.0 gather_fusion.3
  673.7 7.4 scatter.74
  681.1 33.5 %scatter.75 = f32[3,4,130,130]{3,1,0,2:T(4,128)S(1)} dynamic-update-slice(f32[3,4,130,130]{3,1,0,2:T(4,128)S(1)} %scatter.74, f32[3,4,128,1]{3,1,0,2:T(4,128)} %copy.3484, s32[]{:T(128)} %constant.573.clone.1, s32[]{:T(128)} %constant.573.clone.1, s32[]{:T(128)} %constant.575.clone.1, s32[]{:T(128)} %constant.579.clone.1) | dynamic-update-slice | bytes 12292 | tf_op jit(solution)/shard_map/scatter | solution.py:53
  720.9 18.7 %all_gather.46 = f32[4,3,128,128]{3,2,1,0:T(8,128)S(1)} all-gather(f32[1,3,128,128]{3,2,1,0:T(8,128)S(1)} %fusion.74), channel_id=1, replica_groups=mesh['tile'=64,'lev'=4] {'lev'}, dimensions={0}, use_global_device_ids=true | all-gather | bytes 983040 | tf_op jit(solution)/shard_map/all_gather | solution.py:14
  (218 shorter events, 61.8 us)
Async XLA Ops:
  6.5 4.4 copy-start
  6.5 112.9 %all-gather.10.cloned.1.call-start = ((), (), s32[]{:S(2)}) async-start(), calls=%async_computation | async-start | bytes 1597440 | tf_op jit(solution)/shard_map/all_gather | solution.py:117
  9.0 2.2 copy-start.24
  9.0 2.2 copy-start.25
  9.0 2.4 copy-start.23
  9.0 2.8 copy-start.21
  10.0 291.9 %all-gather.12.cloned.1.call-start = ((), (), s32[]{:S(2)}) async-start(), calls=%async_computation.1 | async-start | bytes 1597440 | tf_op jit(solution)/shard_map/all_gather | solution.py:117
  10.1 18.8 %copy-start.22 = (s32[1,128,128]{2,1,0:T(8,128)S(1)}, s32[1,128,128]{2,1,0:T(8,128)}, u32[]{:S(2)}) copy-start(s32[1,128,128]{2,1,0:T(8,128)} %param.57) | copy-start | bytes 196612
  169.4 1.7 copy-start.1
  169.4 1.7 copy-start.17
  192.8 0.9 copy-start.9
  197.1 287.3 %all-gather.14.cloned.1.call-start = ((), (), s32[]{:S(2)}) async-start(), calls=%async_computation.2 | async-start | bytes 1597440 | tf_op jit(solution)/shard_map/all_gather | solution.py:117
  351.9 1.7 copy-start.2
  351.9 1.7 copy-start.18
  375.2 0.9 copy-start.10
  379.5 287.5 %all-gather.16.cloned.1.call-start = ((), (), s32[]{:S(2)}) async-start(), calls=%async_computation.3 | async-start | bytes 1597440 | tf_op jit(solution)/shard_map/all_gather | solution.py:117
  534.5 1.7 copy-start.3
  534.5 1.7 copy-start.19
  557.8 0.8 copy-start.7
  557.8 0.9 copy-start.11
  717.1 1.7 copy-start.4
  717.1 1.7 copy-start.20
  740.1 0.8 copy-start.8
  740.2 0.9 copy-start.12
  (6 other events, 5.1 us)
Sparse Core Ops, SparseCore 0:
  10.1 109.2 all-gather.9
  197.2 104.6 all-gather.11
  379.6 104.7 all-gather.13
  562.3 104.7 all-gather.15
where the time goes:
time: 759 us; the launch traced here: 749 us
  waiting for transfers between devices  402 us (53%)
  local copies, waits for them, and re-layouts  219 us (29%)
  blocking collectives  91.7 us (12%)
  other arithmetic  21.7 us (3%)
  between operations  14.5 us (2%)
    all_gather x4, waiting for transfers between devices, per_device(): everyone = lax.all_gather(outer_rows[None], 'tile', axis=0, tiled=True)  402 us
    scatter x4, local copies, waits for them, and re-layouts, pad_with(): padded = padded.at[..., 1:-1, -1].set(halo_rows[..., 1, :])  134 us
    all_gather x5, blocking collectives, carried_in(): everything = jax.tree.map(lambda part: lax.all_gather(part, axis), x)  91.7 us
    scatter x4, local copies, waits for them, and re-layouts, pad_with(): padded = padded.at[..., 1:-1, 0].set(halo_rows[..., 0, :])  29.8 us
  transfers between devices with their start and end apart: 4, of which 4 were waited for; matrix products, arithmetic and copies ran while one was open for 1% of the time, Pallas kernels for 0%

commit v1 on v0

v1 whole, which is shorter than its diff:
```python
import functools

import jax
import jax.numpy as jnp
from jax import lax
from jax.experimental import pallas as pl
from jax.experimental.pallas import tpu as pltpu
from jax.sharding import PartitionSpec as P

STEPS = 4
COUPLING = 0.25
SIDE = 128
LEVELS = 4
PLANES = 3 * LEVELS
CHUNKS = 4
ROWS = SIDE // CHUNKS
SUB = 16
TOP = 8
MESH = pl.DeviceIdType.MESH
WEST, EAST, SOUTH, NORTH = range(4)


def distance(x, y):
    return min(x, 4 - x) + min(y, 4 - y)


PLANE = sorted(
    [(x, y, c) for x in range(4) for y in range(4) for c in range(2) if (x, y, c) != (0, 0, 0)],
    key=lambda d: (-distance(d[0], d[1]), -d[2]),
)
PEERS = len(PLANE)


def kernel(
    neighbours, edge_from, rotation, seam_length,
    state_hbm, diffusivity, retention, coriolis, wet_mask,
    out_hbm,
    state, wet, edges, packed, inner, halo, corner_up, corner_down,
    strip_mix, strip_keep, strip_spin, strip_wet,
    turn_cos, turn_sin, inside, flips,
    columns, chosen, sending, arrived, partner, gathered, theirs, carry_out, carry_in, strip_out, strip_in,
    load_sem, send_sem, arrive_sem, partner_send, partner_arrive,
    carry_send, carry_arrive, strip_send, strip_arrive,
):
    me = lax.axis_index("tile")
    lev = lax.axis_index("lev")
    px, py, pz, pc = me // 16, (me // 4) % 4, (me // 2) % 2, me % 2
    across = ((px * 4 + py) * 2 + (1 - pz)) * 2 + pc
    down, up = (lev + 3) % 4, (lev + 1) % 4
    half = COUPLING * 0.5

    def peer(d):
        return (((px + d[0]) % 4 * 4 + (py + d[1]) % 4) * 2 + pz) * 2 + (pc + d[2]) % 2

    load = pltpu.make_async_copy(state_hbm, state.at[0, :, :, pl.ds(TOP, SIDE)], load_sem)
    load.start()

    barrier = pltpu.get_barrier_semaphore()
    pl.semaphore_signal(barrier, inc=1, device_id={"tile": across}, device_id_type=MESH)
    for d in PLANE:
        pl.semaphore_signal(barrier, inc=1, device_id={"tile": peer(d)}, device_id_type=MESH)
    pl.semaphore_signal(barrier, inc=1, device_id={"lev": up}, device_id_type=MESH)
    pl.semaphore_signal(barrier, inc=1, device_id={"lev": down}, device_id_type=MESH)

    def choose(k, _):
        t = (k // 2) * 4 + pz * 2 + k % 2
        mine, theirs = jnp.int32(0), jnp.int32(0)
        for s in range(4):
            source, edge = neighbours[t, s], edge_from[t, s]
            mine = mine + jnp.where(source == me, edge, 0)
            theirs = theirs + jnp.where(source == across, edge, 0)
        chosen[0, t] = mine
        chosen[1, t] = theirs
        return 0

    lax.fori_loop(0, 32, choose, 0)

    lane4 = lax.broadcasted_iota(jnp.int32, (4, SIDE), 1)
    edge4 = lax.broadcasted_iota(jnp.int32, (4, SIDE), 0)
    lane_sub = lax.broadcasted_iota(jnp.int32, (ROWS, SIDE), 1)
    for s in range(4):
        turn = rotation[me, s]
        cells = seam_length[me, s]
        cosine = (turn == 0).astype(jnp.float32) - (turn == 2).astype(jnp.float32)
        sine = (turn == 1).astype(jnp.float32) - (turn == 3).astype(jnp.float32)
        flip = (turn == 1).astype(jnp.int32) + (turn == 2).astype(jnp.int32)
        within = jnp.where(lane4 < cells, 1.0, 0.0).astype(jnp.float32)
        inside[s] = within
        turn_cos[s] = within * cosine
        turn_sin[s] = within * sine
        flips[s] = jnp.zeros((4, SIDE), jnp.int32) + flip

    wet[...] = wet_mask[...].astype(jnp.float32)

    def transposed(read, count, first, last):
        for b in range(CHUNKS):
            found = jnp.zeros((ROWS, SIDE), jnp.float32)
            for p in range(count):
                value = pltpu.roll(read(p, b), (2 * p - first) % SIDE, 1)
                here = (lane_sub == 2 * p) | (lane_sub == (2 * p - first + last) % SIDE)
                found = jnp.where(here, value, found)
            columns[pl.ds(b * ROWS, ROWS), :] = found
        columns[...] = columns[...].T

    def row_of(p, first, last):
        return (2 * p - first + last) % SIDE

    def coefficient(p, b):
        rows = pl.ds(b * ROWS, ROWS)
        if p < LEVELS:
            return diffusivity[p, rows, :]
        if p < 2 * LEVELS:
            return retention[p - LEVELS, rows, :]
        return coriolis[rows, :] if p == 2 * LEVELS else wet[rows, :]

    transposed(coefficient, 2 * LEVELS + 2, 0, SIDE - 1)
    for p in range(2 * LEVELS + 2):
        if p < LEVELS:
            target, source = strip_mix.at[p], diffusivity.at[p]
        elif p < 2 * LEVELS:
            target, source = strip_keep.at[p - LEVELS], retention.at[p - LEVELS]
        else:
            target, source = (strip_spin, coriolis) if p == 2 * LEVELS else (strip_wet, wet)
        target[pl.ds(WEST, 1), :] = columns[pl.ds(2 * p, 1), :]
        target[pl.ds(EAST, 1), :] = columns[pl.ds(row_of(p, 0, SIDE - 1), 1), :]
        target[pl.ds(SOUTH, 1), :] = source[pl.ds(0, 1), :]
        target[pl.ds(NORTH, 1), :] = source[pl.ds(SIDE - 1, 1), :]

    load.wait()

    def plane_rows(now):
        return lambda p, b: state[now, p // LEVELS, p % LEVELS, pl.ds(TOP + b * ROWS, ROWS), :]

    transposed(plane_rows(0), PLANES, 0, SIDE - 1)
    for p in range(PLANES):
        c, l = p // LEVELS, p % LEVELS
        edges[c, l, pl.ds(WEST, 1), :] = columns[pl.ds(2 * p, 1), :]
        edges[c, l, pl.ds(EAST, 1), :] = columns[pl.ds(row_of(p, 0, SIDE - 1), 1), :]
        edges[c, l, pl.ds(SOUTH, 1), :] = state[0, c, l, pl.ds(TOP, 1), :]
        edges[c, l, pl.ds(NORTH, 1), :] = state[0, c, l, pl.ds(TOP + SIDE - 1, 1), :]
    for e in range(4):
        for c in range(3):
            packed[e, c] = edges[c, :, e, :]

    pl.semaphore_wait(barrier, PEERS + 3)

    def settle_edges(now):
        for p in range(PLANES):
            c, l = p // LEVELS, p % LEVELS
            columns[pl.ds(2 * p, 1), :] = edges[c, l, pl.ds(WEST, 1), :]
            columns[pl.ds(row_of(p, 0, SIDE - 1), 1), :] = edges[c, l, pl.ds(EAST, 1), :]
            state[now, c, l, pl.ds(TOP, 1), :] = edges[c, l, pl.ds(SOUTH, 1), :]
            state[now, c, l, pl.ds(TOP + SIDE - 1, 1), :] = edges[c, l, pl.ds(NORTH, 1), :]
        columns[...] = columns[...].T
        for b in range(CHUNKS):
            turned = columns[pl.ds(b * ROWS, ROWS), :]
            found = jnp.zeros((ROWS, SIDE), jnp.float32)
            for p in range(PLANES):
                c, l = p // LEVELS, p % LEVELS
                rows = pl.ds(TOP + b * ROWS, ROWS)
                rim = pltpu.roll(turned, (-2 * p) % SIDE, 1)
                value = jnp.where(
                    (lane_sub == 0) | (lane_sub == SIDE - 1), rim, state[now, c, l, rows, :]
                )
                state[now, c, l, rows, :] = value
                here = (lane_sub == 2 * p) | (lane_sub == row_of(p, 1, SIDE - 2))
                found = jnp.where(here, pltpu.roll(value, (2 * p - 1) % SIDE, 1), found)
            columns[pl.ds(b * ROWS, ROWS), :] = found
        columns[...] = columns[...].T
        for p in range(PLANES):
            c, l = p // LEVELS, p % LEVELS
            inner[c, l, pl.ds(WEST, 1), :] = columns[pl.ds(2 * p, 1), :]
            inner[c, l, pl.ds(EAST, 1), :] = columns[pl.ds(row_of(p, 1, SIDE - 2), 1), :]
            inner[c, l, pl.ds(SOUTH, 1), :] = state[now, c, l, pl.ds(TOP + 1, 1), :]
            inner[c, l, pl.ds(NORTH, 1), :] = state[now, c, l, pl.ds(TOP + SIDE - 2, 1), :]

    def carry_copy(r, j):
        return pltpu.make_async_remote_copy(
            carry_out.at[r, j], carry_in.at[r, j], carry_send.at[r, j], carry_arrive.at[r, j],
            device_id={"lev": down}, device_id_type=MESH,
        )

    def strip_copy(r):
        return pltpu.make_async_remote_copy(
            strip_out.at[r], strip_in.at[r], strip_send.at[r], strip_arrive.at[r],
            device_id={"lev": down}, device_id_type=MESH,
        )

    def partner_copy(r):
        return pltpu.make_async_remote_copy(
            packed, partner.at[r], partner_send.at[r], partner_arrive.at[r],
            device_id={"tile": across}, device_id_type=MESH,
        )

    def send(r, k, d, slot):
        pltpu.make_async_remote_copy(
            sending.at[k], arrived.at[r, slot], send_sem.at[r], arrive_sem.at[r],
            device_id={"tile": peer(d)}, device_id_type=MESH,
        ).start()

    def bulk(r, now, later, j):
        @pl.when(lev < 3)
        def _():
            carry_copy(r, j).wait_recv()

        for b in range(ROWS // SUB):
            at = j * ROWS + b * SUB
            cells = pl.ds(at, SUB)
            spin, dry = coriolis[cells, :], wet[cells, :]
            below = [
                jnp.where(lev == 3, 0.0, carry_in[r, j, c, pl.ds(b * SUB, SUB), :]) for c in range(3)
            ]
            for l in range(LEVELS - 1, -1, -1):
                mid = [state[now, c, l, pl.ds(TOP + at, SUB), :] for c in range(3)]
                north = [state[now, c, l, pl.ds(TOP + at + 1, SUB), :] for c in range(3)]
                south = [state[now, c, l, pl.ds(TOP + at - 1, SUB), :] for c in range(3)]
                east = [pltpu.roll(f, SIDE - 1, 1) for f in mid]
                west = [pltpu.roll(f, 1, 1) for f in mid]
                mix, keep = diffusivity[l, cells, :], retention[l, cells, :]
                spread = [
                    mid[c] + mix * (east[c] + west[c] + north[c] + south[c] - 4.0 * mid[c])
                    for c in range(3)
                ]
                fresh = [
                    spread[0] - half * ((east[1] - west[1]) + (north[2] - south[2])),
                    spread[1] - half * (east[0] - west[0]) + spin * mid[2],
                    spread[2] - half * (north[0] - south[0]) - spin * mid[1],
                ]
                open_keep = (1.0 - keep) * dry
                below = [open_keep * fresh[c] + keep * below[c] for c in range(3)]
                for c in range(3):
                    state[later, c, l, pl.ds(TOP + at, SUB), :] = below[c]
            for c in range(3):
                carry_out[r, j, c, pl.ds(b * SUB, SUB), :] = below[c]

        @pl.when(lev > 0)
        def _():
            carry_copy(r, j).start()

    def advance_edges(r):
        for s in range(4):
            source = neighbours[me, s]
            strip = gathered[source]
            turned = []
            for c in range(3):
                mirrored = jnp.take_along_axis(strip[c], SIDE - 1 - lane4, axis=1)
                turned.append(jnp.where(flips[s] > 0, mirrored, strip[c]))
            around = [
                turned[0] * inside[s],
                turn_cos[s] * turned[1] + turn_sin[s] * turned[2],
                turn_cos[s] * turned[2] - turn_sin[s] * turned[1],
            ]
            for c in range(3):
                halo[c, :, s, :] = around[c]
                if s == NORTH or s == EAST:
                    first = 0 if s == NORTH else 2
                    corner_up[c, :, first, :] = around[c]
                    corner_up[c, :, first + 1, :] = around[c]
                else:
                    first = 0 if s == SOUTH else 2
                    corner_down[c, :, first, :] = around[c]
                    corner_down[c, :, first + 1, :] = around[c]

        sides = edge4 < 2
        leading = (edge4 == WEST) | (edge4 == SOUTH)
        sign = jnp.where(leading, 1.0, -1.0).astype(jnp.float32)
        spin, dry = strip_spin[...], strip_wet[...]

        @pl.when(lev < 3)
        def _():
            strip_copy(r).wait_recv()

        below = [jnp.where(lev == 3, 0.0, strip_in[r, c]) for c in range(3)]
        for l in range(LEVELS - 1, -1, -1):
            mid = [edges[c, l] for c in range(3)]
            total, by_x, by_y = [], [], []
            for c in range(3):
                above, beneath = corner_up[c, l], corner_down[c, l]
                far = jnp.where(leading, pltpu.roll(above, SIDE - 1, 1), above)
                near = jnp.where(leading, beneath, pltpu.roll(beneath, 1, 1))
                ahead = jnp.where(lane4 == SIDE - 1, far, pltpu.roll(mid[c], SIDE - 1, 1))
                behind = jnp.where(lane4 == 0, near, pltpu.roll(mid[c], 1, 1))
                outer, within = halo[c, l], inner[c, l]
                total.append(outer + within + ahead + behind)
                through = sign * (within - outer)
                along = ahead - behind
                by_x.append(jnp.where(sides, through, along))
                by_y.append(jnp.where(sides, along, through))
            mix, keep = strip_mix[l], strip_keep[l]
            spread = [mid[c] + mix * (total[c] - 4.0 * mid[c]) for c in range(3)]
            fresh = [
                spread[0] - half * (by_x[1] + by_y[2]),
                spread[1] - half * by_x[0] + spin * mid[2],
                spread[2] - half * by_y[0] - spin * mid[1],
            ]
            open_keep = (1.0 - keep) * dry
            below = [open_keep * fresh[c] + keep * below[c] for c in range(3)]
            for c in range(3):
                edges[c, l] = below[c]
        for c in range(3):
            strip_out[r, c] = below[c]

        @pl.when(lev > 0)
        def _():
            strip_copy(r).start()

        for e in range(4):
            for c in range(3):
                packed[e, c] = edges[c, :, e, :]

    def step(r, _):
        now, later = r % 2, (r + 1) % 2
        partner_copy(r).start()
        for k, d in enumerate(PLANE):
            sending[k] = packed[chosen[0, peer(d)]]
            send(r, k, d, me)
        settle_edges(now)
        bulk(r, now, later, 0)
        partner_copy(r).wait()
        theirs[...] = partner[r]
        for k, d in enumerate(PLANE):
            sending[PEERS + k] = theirs[chosen[1, peer(d)]]
            send(r, PEERS + k, d, across)
        for j in range(1, CHUNKS):
            bulk(r, now, later, j)
        everyone = arrived.at[r, pl.ds(0, 2 * PEERS)]
        pltpu.make_async_remote_copy(
            everyone, everyone, send_sem.at[r], arrive_sem.at[r],
            device_id={"tile": across}, device_id_type=MESH,
        ).wait()
        gathered[...] = arrived[r]
        gathered[across] = theirs[chosen[1, me]]
        advance_edges(r)
        return 0

    lax.fori_loop(0, STEPS, step, 0)
    settle_edges(STEPS % 2)
    store = pltpu.make_async_copy(
        state.at[STEPS % 2, :, :, pl.ds(TOP, SIDE)], out_hbm, load_sem
    )
    store.start()

    @pl.when(lev > 0)
    def _():
        def drain(r, _):
            for j in range(CHUNKS):
                carry_copy(r, j).wait_send()
            strip_copy(r).wait_send()
            return 0

        lax.fori_loop(0, STEPS, drain, 0)

    store.wait()


def per_device(
    adjoint_state, diffusivity, retention, coriolis,
    neighbours, edge_from, rotation, seam_length, wet_mask,
):
    tiles = neighbours.shape[0]
    f32 = jnp.float32
    vmem, dma = pltpu.VMEM, pltpu.SemaphoreType.DMA
    strips = (3, LEVELS, 4, SIDE)
    small = pl.BlockSpec(memory_space=pltpu.SMEM)
    fast = pl.BlockSpec(memory_space=pltpu.VMEM)
    anywhere = pl.BlockSpec(memory_space=pl.ANY)
    out = pl.pallas_call(
        kernel,
        out_shape=jax.ShapeDtypeStruct((3, LEVELS, SIDE, SIDE), f32),
        in_specs=[small] * 4 + [anywhere] + [fast] * 4,
        out_specs=anywhere,
        scratch_shapes=[
            vmem((2, 3, LEVELS, SIDE + 2 * TOP, SIDE), f32),
            vmem((SIDE, SIDE), f32),
            vmem(strips, f32),
            vmem((4, 3, LEVELS, SIDE), f32),
            vmem(strips, f32),
            vmem(strips, f32),
            vmem(strips, f32),
            vmem(strips, f32),
            vmem((LEVELS, 4, SIDE), f32),
            vmem((LEVELS, 4, SIDE), f32),
            vmem((4, SIDE), f32),
            vmem((4, SIDE), f32),
            vmem((4, 4, SIDE), f32),
            vmem((4, 4, SIDE), f32),
            vmem((4, 4, SIDE), f32),
            vmem((4, 4, SIDE), jnp.int32),
            vmem((SIDE, SIDE), f32),
            pltpu.SMEM((2, tiles), jnp.int32),
            vmem((2 * PEERS, 3, LEVELS, SIDE), f32),
            vmem((STEPS, tiles, 3, LEVELS, SIDE), f32),
            vmem((STEPS, 4, 3, LEVELS, SIDE), f32),
            vmem((tiles, 3, LEVELS, SIDE), f32),
            vmem((4, 3, LEVELS, SIDE), f32),
            vmem((STEPS, CHUNKS, 3, ROWS, SIDE), f32),
            vmem((STEPS, CHUNKS, 3, ROWS, SIDE), f32),
            vmem((STEPS, 3, 4, SIDE), f32),
            vmem((STEPS, 3, 4, SIDE), f32),
            dma,
            dma((STEPS,)),
            dma((STEPS,)),
            dma((STEPS,)),
            dma((STEPS,)),
            dma((STEPS, CHUNKS)),
            dma((STEPS, CHUNKS)),
            dma((STEPS,)),
            dma((STEPS,)),
        ],
        compiler_params=pltpu.CompilerParams(
            collective_id=0, has_side_effects=True, vmem_limit_bytes=32 << 20
        ),
    )(
        neighbours, edge_from, rotation, seam_length,
        adjoint_state[:, :, 0], diffusivity[:, 0], retention[:, 0], coriolis[0], wet_mask[0],
    )
    return out[:, :, None]


def solution(mesh):
    in_specs = (
        P(None, "lev", "tile", None, None),
        P("lev", "tile", None, None),
        P("lev", "tile", None, None),
        P("tile", None, None),
        P(),
        P(),
        P(),
        P(),
        P("tile", None, None),
    )
    out_specs = P(None, "lev", "tile", None, None)
    return jax.shard_map(
        per_device, mesh=mesh, in_specs=in_specs, out_specs=out_specs, check_vma=False
    )
```

time: 759 us -> 77.5 us (0.10); the launches traced: 749 us -> 77.2 us
  waiting for transfers between devices: 402 us -> 0 us
  local copies, waits for them, and re-layouts: 219 us -> 5.45 us
  blocking collectives: 91.7 us -> 0 us
  Pallas kernels: 0 us -> 71.7 us
  other arithmetic: 21.7 us -> 0 us
  between operations: 14.5 us -> 0.03 us
    all_gather x4 -> x0, waiting for transfers between devices: 402 us -> none  [per_device(): everyone = lax.all_gather(outer_rows[None], 'tile', axis=0, tiled=True)]
    scatter x16 -> x0, local copies, waits for them, and re-layouts: 173 us -> none  [the longest x4 134 us: pad_with(): padded = padded.at[..., 1:-1, -1].set(halo_rows[..., 1, :])]
    all_gather x5 -> x0, blocking collectives: 91.7 us -> none  [carried_in(): everything = jax.tree.map(lambda part: lax.all_gather(part, axis), x)]
    pallas_call x0 -> x1, Pallas kernels: none -> 71.7 us  [per_device(): pl.pallas_call(kernel, out_shape=jax.ShapeDtypeStruct((3, LEVELS, SIDE, S...]
    all_gather x4 -> x0, local copies, waits for them, and re-layouts: 11.3 us -> none  [per_device(): everyone = lax.all_gather(outer_rows[None], 'tile', axis=0, tiled=True)]
    another operation x22 -> x0, local copies, waits for them, and re-layouts: 9.27 us -> none
    gather x4 -> x0, local copies, waits for them, and re-layouts: 7.95 us -> none  [per_device(): picked = jnp.moveaxis(everyone[neighbour_row, :, :, source_row, :], 0, 2)]
  transfers between devices with their start and end apart: 4 -> 0, of which waited for: 4 -> 0; matrix products, arithmetic and copies ran while one was open for 1% -> 0% of each run, Pallas kernels for 0% -> 0%
where the time goes in v1:
time: 77.5 us; the launch traced here: 77.2 us
  Pallas kernels  71.7 us (93%)
  local copies, waits for them, and re-layouts  5.45 us (7%)
    pallas_call x1, Pallas kernels, per_device(): pl.pallas_call(kernel, out_shape=jax.ShapeDtypeStruct((3, LEVELS, SIDE, S...  71.7 us
    unnamed x23, local copies, waits for them, and re-layouts  5.45 us

profile of v1, /device:TPU:1, one launch (start us, length us, event | category | flops | bytes accessed | tf_op | source)
XLA Modules:
  0.0 77.2 jit_solution(16132977072287433879)
XLA Ops:
  0.0 0.0 copy-start.5
  0.0 0.0 copy-start.6
  0.0 0.0 copy-start.7
  0.0 0.0 copy-start.8
  0.0 0.7 copy-done.5
  0.7 0.0 copy-start.3
  0.7 0.0 copy-start.4
  0.7 0.1 copy.10.neighbours
  0.8 0.0 copy-done.6
  0.8 0.1 copy.11.edge_from
  0.9 0.0 copy-done.7
  0.9 0.1 copy.12.rotation
  1.0 0.0 copy-done.8
  1.0 0.1 copy.13.seam_length
  1.1 0.4 copy-done.3
  1.5 0.0 copy-done.4
  1.6 0.0 copy-start
  1.6 1.1 %copy-done = f32[3,4,1,128,128]{4,3,2,1,0:T(8,128)S(1)} copy-done((f32[3,4,1,128,128]{4,3,2,1,0:T(8,128)S(1)}, f32[3,4,1,128,128]{4,3,2,1,0:T(8,128)}, u32[]{:S(2)}) %copy-start) | copy-done | bytes 786456
  2.7 0.0 copy-start.1
  2.7 0.9 %copy-done.1 = f32[4,1,128,128]{3,2,1,0:T(8,128)S(1)} copy-done((f32[4,1,128,128]{3,2,1,0:T(8,128)S(1)}, f32[4,1,128,128]{3,2,1,0:T(8,128)}, u32[]{:S(2)}) %copy-start.1) | copy-done | bytes 262168
  3.6 0.0 copy-start.2
  3.6 0.9 %copy-done.2 = f32[4,1,128,128]{3,2,1,0:T(8,128)S(1)} copy-done((f32[4,1,128,128]{3,2,1,0:T(8,128)S(1)}, f32[4,1,128,128]{3,2,1,0:T(8,128)}, u32[]{:S(2)}) %copy-start.2) | copy-done | bytes 262168
  4.6 71.7 %shard_map.91 = f32[3,4,128,128]{3,2,1,0:T(8,128)S(1)} custom-call(s32[64,4]{1,0:T(8,128)S(1)} %copy.10.neighbours, s32[64,4]{1,0:T(8,128)S(1)} %copy.11.edge_from, s32[64,4]{1,0:T(8,128)S(1)} %copy.12.rotation, s32[64,4]{1,0:T(8,128)S(1)} %copy.13.seam_length, f32[3,4,128,128]{3,2,1,0:T(8,128)S(1)} %bitcast.9, f32[4,128,128]{2,1,0:T(8,128)S(1)} %bitcast.10, ...), custom_call_target="tpu_custom_call" | custom-call | tf_op jit(solution)/shard_map/pallas_call | solution.py:367
  76.3 0.9 %copy.16 = f32[3,4,1,128,128]{4,3,2,1,0:T(8,128)} copy(f32[3,4,1,128,128]{4,3,2,1,0:T(8,128)S(1)} %bitcast.8) | data formatting | bytes 1572864
Async XLA Ops:
  0.0 0.7 copy-start.5
  0.0 0.8 %copy-start.6 = (s32[64,4]{0,1:T(4,128)S(1)}, s32[64,4]{0,1:T(4,128)}, u32[]{:S(2)}) copy-start(s32[64,4]{0,1:T(4,128)} %param.14) | copy-start | bytes 3076
  0.0 0.9 %copy-start.7 = (s32[64,4]{0,1:T(4,128)S(1)}, s32[64,4]{0,1:T(4,128)}, u32[]{:S(2)}) copy-start(s32[64,4]{0,1:T(4,128)} %param.15) | copy-start | bytes 3076
  0.0 1.0 %copy-start.8 = (s32[64,4]{0,1:T(4,128)S(1)}, s32[64,4]{0,1:T(4,128)}, u32[]{:S(2)}) copy-start(s32[64,4]{0,1:T(4,128)} %param.16) | copy-start | bytes 3076
  0.7 0.8 %copy-start.3 = (f32[1,128,128]{2,1,0:T(8,128)S(1)}, f32[1,128,128]{2,1,0:T(8,128)}, u32[]{:S(2)}) copy-start(f32[1,128,128]{2,1,0:T(8,128)} %param.12) | copy-start | bytes 196612
  0.7 0.9 %copy-start.4 = (s32[1,128,128]{2,1,0:T(8,128)S(1)}, s32[1,128,128]{2,1,0:T(8,128)}, u32[]{:S(2)}) copy-start(s32[1,128,128]{2,1,0:T(8,128)} %param.17) | copy-start | bytes 196612
  1.6 1.1 %copy-start = (f32[3,4,1,128,128]{4,3,2,1,0:T(8,128)S(1)}, f32[3,4,1,128,128]{4,3,2,1,0:T(8,128)}, u32[]{:S(2)}) copy-start(f32[3,4,1,128,128]{4,3,2,1,0:T(8,128)} %param.9) | copy-start | bytes 2359300
  2.7 0.9 %copy-start.1 = (f32[4,1,128,128]{3,2,1,0:T(8,128)S(1)}, f32[4,1,128,128]{3,2,1,0:T(8,128)}, u32[]{:S(2)}) copy-start(f32[4,1,128,128]{3,2,1,0:T(8,128)} %param.10) | copy-start | bytes 786436
  3.6 0.9 %copy-start.2 = (f32[4,1,128,128]{3,2,1,0:T(8,128)S(1)}, f32[4,1,128,128]{3,2,1,0:T(8,128)}, u32[]{:S(2)}) copy-start(f32[4,1,128,128]{3,2,1,0:T(8,128)} %param.11) | copy-start | bytes 786436

commit v2 on v1

--- a/solution.py
+++ b/solution.py
@@ -13,6 +13,8 @@
 LEVELS = 4
 PLANES = 3 * LEVELS
 CHUNKS = 4
+FIRST = 1
+EARLY = 4
 ROWS = SIDE // CHUNKS
 SUB = 16
 TOP = 8
@@ -33,13 +35,13 @@
 
 def kernel(
     neighbours, edge_from, rotation, seam_length,
-    state_hbm, diffusivity, retention, coriolis, wet_mask,
+    state_hbm, diffusivity_hbm, retention_hbm, coriolis_hbm, wet_hbm,
     out_hbm,
-    state, wet, edges, packed, inner, halo, corner_up, corner_down,
+    state, diffusivity, retention, coriolis, wet_mask, wet, edges, packed, inner, halo, corner_up, corner_down,
     strip_mix, strip_keep, strip_spin, strip_wet,
     turn_cos, turn_sin, inside, flips,
     columns, chosen, sending, arrived, partner, gathered, theirs, carry_out, carry_in, strip_out, strip_in,
-    load_sem, send_sem, arrive_sem, partner_send, partner_arrive,
+    load_sem, coefficient_sem, send_sem, arrive_sem, partner_send, partner_arrive,
     carry_send, carry_arrive, strip_send, strip_arrive,
 ):
     me = lax.axis_index("tile")
@@ -53,6 +55,17 @@
         return (((px + d[0]) % 4 * 4 + (py + d[1]) % 4) * 2 + pz) * 2 + (pc + d[2]) % 2
 
     load = pltpu.make_async_copy(state_hbm, state.at[0, :, :, pl.ds(TOP, SIDE)], load_sem)
+    loads = [
+        pltpu.make_async_copy(source, target, coefficient_sem.at[i])
+        for i, (source, target) in enumerate(
+            [
+                (diffusivity_hbm, diffusivity), (retention_hbm, retention),
+                (coriolis_hbm, coriolis), (wet_hbm, wet_mask),
+            ]
+        )
+    ]
+    for copy in loads:
+        copy.start()
     load.start()
 
     barrier = pltpu.get_barrier_semaphore()
@@ -66,7 +79,7 @@
         t = (k // 2) * 4 + pz * 2 + k % 2
         mine, theirs = jnp.int32(0), jnp.int32(0)
         for s in range(4):
-            source, edge = neighbours[t, s], edge_from[t, s]
+            source, edge = neighbours[s, t], edge_from[s, t]
             mine = mine + jnp.where(source == me, edge, 0)
             theirs = theirs + jnp.where(source == across, edge, 0)
         chosen[0, t] = mine
@@ -79,8 +92,8 @@
     edge4 = lax.broadcasted_iota(jnp.int32, (4, SIDE), 0)
     lane_sub = lax.broadcasted_iota(jnp.int32, (ROWS, SIDE), 1)
     for s in range(4):
-        turn = rotation[me, s]
-        cells = seam_length[me, s]
+        turn = rotation[s, me]
+        cells = seam_length[s, me]
         cosine = (turn == 0).astype(jnp.float32) - (turn == 2).astype(jnp.float32)
         sine = (turn == 1).astype(jnp.float32) - (turn == 3).astype(jnp.float32)
         flip = (turn == 1).astype(jnp.int32) + (turn == 2).astype(jnp.int32)
@@ -90,6 +103,8 @@
         turn_sin[s] = within * sine
         flips[s] = jnp.zeros((4, SIDE), jnp.int32) + flip
 
+    for copy in loads:
+        copy.wait()
     wet[...] = wet_mask[...].astype(jnp.float32)
 
     def transposed(read, count, first, last):
@@ -198,7 +213,9 @@
             device_id={"tile": peer(d)}, device_id_type=MESH,
         ).start()
 
-    def bulk(r, now, later, j):
+    def bulk(r, j):
+        now, later = r % 2, (r + 1) % 2
+
         @pl.when(lev < 3)
         def _():
             carry_copy(r, j).wait_recv()
@@ -239,7 +256,7 @@
 
     def advance_edges(r):
         for s in range(4):
-            source = neighbours[me, s]
+            source = neighbours[s, me]
             strip = gathered[source]
             turned = []
             for c in range(3):
@@ -266,11 +283,7 @@
         sign = jnp.where(leading, 1.0, -1.0).astype(jnp.float32)
         spin, dry = strip_spin[...], strip_wet[...]
 
-        @pl.when(lev < 3)
-        def _():
-            strip_copy(r).wait_recv()
-
-        below = [jnp.where(lev == 3, 0.0, strip_in[r, c]) for c in range(3)]
+        grown = [None] * LEVELS
         for l in range(LEVELS - 1, -1, -1):
             mid = [edges[c, l] for c in range(3)]
             total, by_x, by_y = [], [], []
@@ -294,7 +307,15 @@
                 spread[2] - half * by_y[0] - spin * mid[1],
             ]
             open_keep = (1.0 - keep) * dry
-            below = [open_keep * fresh[c] + keep * below[c] for c in range(3)]
+            grown[l] = [open_keep * fresh[c] for c in range(3)]
+
+        @pl.when(lev < 3)
+        def _():
+            strip_copy(r).wait_recv()
+
+        below = [jnp.where(lev == 3, 0.0, strip_in[r, c]) for c in range(3)]
+        for l in range(LEVELS - 1, -1, -1):
+            below = [grown[l][c] + strip_keep[l] * below[c] for c in range(3)]
             for c in range(3):
                 edges[c, l] = below[c]
         for c in range(3):
@@ -309,20 +330,26 @@
                 packed[e, c] = edges[c, :, e, :]
 
     def step(r, _):
-        now, later = r % 2, (r + 1) % 2
         partner_copy(r).start()
         for k, d in enumerate(PLANE):
             sending[k] = packed[chosen[0, peer(d)]]
             send(r, k, d, me)
-        settle_edges(now)
-        bulk(r, now, later, 0)
+
+        @pl.when(r > 0)
+        def _():
+            for j in range(EARLY, CHUNKS):
+                bulk(r - 1, j)
+
+        settle_edges(r % 2)
+        for j in range(FIRST):
+            bulk(r, j)
         partner_copy(r).wait()
         theirs[...] = partner[r]
         for k, d in enumerate(PLANE):
             sending[PEERS + k] = theirs[chosen[1, peer(d)]]
             send(r, PEERS + k, d, across)
-        for j in range(1, CHUNKS):
-            bulk(r, now, later, j)
+        for j in range(FIRST, EARLY):
+            bulk(r, j)
         everyone = arrived.at[r, pl.ds(0, 2 * PEERS)]
         pltpu.make_async_remote_copy(
             everyone, everyone, send_sem.at[r], arrive_sem.at[r],
@@ -334,6 +361,8 @@
         return 0
 
     lax.fori_loop(0, STEPS, step, 0)
+    for j in range(EARLY, CHUNKS):
+        bulk(STEPS - 1, j)
     settle_edges(STEPS % 2)
     store = pltpu.make_async_copy(
         state.at[STEPS % 2, :, :, pl.ds(TOP, SIDE)], out_hbm, load_sem
@@ -362,15 +391,18 @@
     vmem, dma = pltpu.VMEM, pltpu.SemaphoreType.DMA
     strips = (3, LEVELS, 4, SIDE)
     small = pl.BlockSpec(memory_space=pltpu.SMEM)
-    fast = pl.BlockSpec(memory_space=pltpu.VMEM)
-    anywhere = pl.BlockSpec(memory_space=pl.ANY)
+    anywhere = pl.BlockSpec(memory_space=pltpu.HBM)
     out = pl.pallas_call(
         kernel,
         out_shape=jax.ShapeDtypeStruct((3, LEVELS, SIDE, SIDE), f32),
-        in_specs=[small] * 4 + [anywhere] + [fast] * 4,
-        out_specs=anywhere,
+        in_specs=[small] * 4 + [anywhere] * 5,
+        out_specs=pl.BlockSpec(memory_space=pltpu.VMEM),
         scratch_shapes=[
             vmem((2, 3, LEVELS, SIDE + 2 * TOP, SIDE), f32),
+            vmem((LEVELS, SIDE, SIDE), f32),
+            vmem((LEVELS, SIDE, SIDE), f32),
+            vmem((SIDE, SIDE), f32),
+            vmem((SIDE, SIDE), jnp.int32),
             vmem((SIDE, SIDE), f32),
             vmem(strips, f32),
             vmem((4, 3, LEVELS, SIDE), f32),
@@ -398,6 +430,7 @@
             vmem((STEPS, 3, 4, SIDE), f32),
             vmem((STEPS, 3, 4, SIDE), f32),
             dma,
+            dma((4,)),
             dma((STEPS,)),
             dma((STEPS,)),
             dma((STEPS,)),
@@ -408,10 +441,10 @@
             dma((STEPS,)),
         ],
         compiler_params=pltpu.CompilerParams(
-            collective_id=0, has_side_effects=True, vmem_limit_bytes=32 << 20
+            collective_id=0, has_side_effects=True, vmem_limit_bytes=60 << 20
         ),
     )(
-        neighbours, edge_from, rotation, seam_length,
+        neighbours.T, edge_from.T, rotation.T, seam_length.T,
         adjoint_state[:, :, 0], diffusivity[:, 0], retention[:, 0], coriolis[0], wet_mask[0],
     )
     return out[:, :, None]

time: 77.5 us -> 73 us (0.942)
  local copies, waits for them, and re-layouts: 5.45 us -> 2.06 us
  Pallas kernels: 71.7 us -> 70.7 us
    unnamed x23 -> x1, local copies, waits for them, and re-layouts: 5.45 us -> 2.06 us
    pallas_call x1, Pallas kernels: 71.7 us -> 70.7 us  [per_device(): pl.pallas_call(kernel, out_shape=jax.ShapeDtypeStruct((3, LEVELS, SIDE, S...]
where the time goes in v2:
time: 73 us; the launch traced here: 72.8 us
  Pallas kernels  70.7 us (97%)
  local copies, waits for them, and re-layouts  2.06 us (3%)
    pallas_call x1, Pallas kernels, per_device(): pl.pallas_call(kernel, out_shape=jax.ShapeDtypeStruct((3, LEVELS, SIDE, S...  70.7 us
    unnamed x1, local copies, waits for them, and re-layouts  2.06 us

profile of v2, /device:TPU:1, one launch (start us, length us, event | category | flops | bytes accessed | tf_op | source)
XLA Modules:
  0.0 72.8 jit_solution(4896829386183392676)
XLA Ops:
  0.0 70.7 %shard_map.91 = f32[3,4,128,128]{3,2,1,0:T(8,128)} custom-call(s32[4,64]{1,0:T(4,128)} %bitcast.18, s32[4,64]{1,0:T(4,128)} %bitcast.19, s32[4,64]{1,0:T(4,128)} %bitcast.20, s32[4,64]{1,0:T(4,128)} %bitcast.21, f32[3,4,128,128]{3,2,1,0:T(8,128)} %bitcast.13, f32[4,128,128]{2,1,0:T(8,128)} %bitcast.14, f32[4,128,128]{2,1,0:T(8,128)} %bitcast.15, ...), custom_call_target="tpu_custom_call" | custom-call | tf_op jit(solution)/shard_map/pallas_call | solution.py:395
  70.7 2.1 %copy.12 = f32[3,4,1,128,128]{4,3,2,1,0:T(8,128)} copy(f32[3,4,1,128,128]{4,3,2,1,0:T(8,128)} %bitcast.12) | data formatting | bytes 1572864

commit v3 on v2

--- a/solution.py
+++ b/solution.py
@@ -12,9 +12,9 @@
 SIDE = 128
 LEVELS = 4
 PLANES = 3 * LEVELS
-CHUNKS = 4
-FIRST = 1
-EARLY = 4
+CHUNKS = 8
+FIRST = 2
+EARLY = 8
 ROWS = SIDE // CHUNKS
 SUB = 16
 TOP = 8
@@ -252,6 +252,8 @@
 
         @pl.when(lev > 0)
         def _():
+            if j >= 2:
+                carry_copy(r, j - 2).wait_send()
             carry_copy(r, j).start()
 
     def advance_edges(r):
@@ -372,7 +374,7 @@
     @pl.when(lev > 0)
     def _():
         def drain(r, _):
-            for j in range(CHUNKS):
+            for j in range(CHUNKS - 2, CHUNKS):
                 carry_copy(r, j).wait_send()
             strip_copy(r).wait_send()
             return 0

time: 73 us -> 69.5 us (0.952)
  Pallas kernels: 70.7 us -> 67.3 us
    pallas_call x1, Pallas kernels: 70.7 us -> 67.3 us  [per_device(): pl.pallas_call(kernel, out_shape=jax.ShapeDtypeStruct((3, LEVELS, SIDE, S...]
where the time goes in v3:
time: 69.5 us; the launch traced here: 69.3 us
  Pallas kernels  67.3 us (97%)
  local copies, waits for them, and re-layouts  2.06 us (3%)
    pallas_call x1, Pallas kernels, per_device(): pl.pallas_call(kernel, out_shape=jax.ShapeDtypeStruct((3, LEVELS, SIDE, S...  67.3 us
    unnamed x1, local copies, waits for them, and re-layouts  2.06 us

profile of v3, /device:TPU:1, one launch (start us, length us, event | category | flops | bytes accessed | tf_op | source)
XLA Modules:
  0.0 69.3 jit_solution(16059923144391978872)
XLA Ops:
  0.0 67.3 %shard_map.91 = f32[3,4,128,128]{3,2,1,0:T(8,128)} custom-call(s32[4,64]{1,0:T(4,128)} %bitcast.18, s32[4,64]{1,0:T(4,128)} %bitcast.19, s32[4,64]{1,0:T(4,128)} %bitcast.20, s32[4,64]{1,0:T(4,128)} %bitcast.21, f32[3,4,128,128]{3,2,1,0:T(8,128)} %bitcast.13, f32[4,128,128]{2,1,0:T(8,128)} %bitcast.14, f32[4,128,128]{2,1,0:T(8,128)} %bitcast.15, ...), custom_call_target="tpu_custom_call" | custom-call | tf_op jit(solution)/shard_map/pallas_call | solution.py:397
  67.3 2.1 %copy.12 = f32[3,4,1,128,128]{4,3,2,1,0:T(8,128)} copy(f32[3,4,1,128,128]{4,3,2,1,0:T(8,128)} %bitcast.12) | data formatting | bytes 1572864

commit v4 on v3

--- a/solution.py
+++ b/solution.py
@@ -159,7 +159,7 @@
 
     pl.semaphore_wait(barrier, PEERS + 3)
 
-    def settle_edges(now):
+    def settle_edges(now, last=False):
         for p in range(PLANES):
             c, l = p // LEVELS, p % LEVELS
             columns[pl.ds(2 * p, 1), :] = edges[c, l, pl.ds(WEST, 1), :]
@@ -178,9 +178,14 @@
                     (lane_sub == 0) | (lane_sub == SIDE - 1), rim, state[now, c, l, rows, :]
                 )
                 state[now, c, l, rows, :] = value
+                if last:
+                    continue
                 here = (lane_sub == 2 * p) | (lane_sub == row_of(p, 1, SIDE - 2))
                 found = jnp.where(here, pltpu.roll(value, (2 * p - 1) % SIDE, 1), found)
-            columns[pl.ds(b * ROWS, ROWS), :] = found
+            if not last:
+                columns[pl.ds(b * ROWS, ROWS), :] = found
+        if last:
+            return
         columns[...] = columns[...].T
         for p in range(PLANES):
             c, l = p // LEVELS, p % LEVELS
@@ -253,7 +258,9 @@
         @pl.when(lev > 0)
         def _():
             if j >= 2:
-                carry_copy(r, j - 2).wait_send()
+                @pl.when(r < STEPS - 1)
+                def _():
+                    carry_copy(r, j - 2).wait_send()
             carry_copy(r, j).start()
 
     def advance_edges(r):
@@ -365,7 +372,7 @@
     lax.fori_loop(0, STEPS, step, 0)
     for j in range(EARLY, CHUNKS):
         bulk(STEPS - 1, j)
-    settle_edges(STEPS % 2)
+    settle_edges(STEPS % 2, last=True)
     store = pltpu.make_async_copy(
         state.at[STEPS % 2, :, :, pl.ds(TOP, SIDE)], out_hbm, load_sem
     )
@@ -380,6 +387,8 @@
             return 0
 
         lax.fori_loop(0, STEPS, drain, 0)
+        for j in range(CHUNKS - 2):
+            carry_copy(STEPS - 1, j).wait_send()
 
     store.wait()
 

time: 69.5 us -> 67.6 us (0.973)
  Pallas kernels: 67.3 us -> 65.3 us
    pallas_call x1, Pallas kernels: 67.3 us -> 65.3 us  [per_device(): pl.pallas_call(kernel, out_shape=jax.ShapeDtypeStruct((3, LEVELS, SIDE, S...]
where the time goes in v4:
time: 67.6 us; the launch traced here: 67.4 us
  Pallas kernels  65.3 us (97%)
  local copies, waits for them, and re-layouts  2.06 us (3%)
    pallas_call x1, Pallas kernels, per_device(): pl.pallas_call(kernel, out_shape=jax.ShapeDtypeStruct((3, LEVELS, SIDE, S...  65.3 us
    unnamed x1, local copies, waits for them, and re-layouts  2.06 us

profile of v4, /device:TPU:1, one launch (start us, length us, event | category | flops | bytes accessed | tf_op | source)
XLA Modules:
  0.0 67.4 jit_solution(16464206501977170198)
XLA Ops:
  0.0 65.3 %shard_map.91 = f32[3,4,128,128]{3,2,1,0:T(8,128)} custom-call(s32[4,64]{1,0:T(4,128)} %bitcast.18, s32[4,64]{1,0:T(4,128)} %bitcast.19, s32[4,64]{1,0:T(4,128)} %bitcast.20, s32[4,64]{1,0:T(4,128)} %bitcast.21, f32[3,4,128,128]{3,2,1,0:T(8,128)} %bitcast.13, f32[4,128,128]{2,1,0:T(8,128)} %bitcast.14, f32[4,128,128]{2,1,0:T(8,128)} %bitcast.15, ...), custom_call_target="tpu_custom_call" | custom-call | tf_op jit(solution)/shard_map/pallas_call | solution.py:406
  65.4 2.1 %copy.12 = f32[3,4,1,128,128]{4,3,2,1,0:T(8,128)} copy(f32[3,4,1,128,128]{4,3,2,1,0:T(8,128)} %bitcast.12) | data formatting | bytes 1572864
